TPU v7x, 512 devices: a whole 4x8x8 slice. The times are simulated.
512 devices in a mesh: req: 128 (over z, y, core), head: 4 (over x).
Axes of the slice: x: 4, y: 8, z: 8, core: 2. Of those that a mesh axis runs over, the one named last changes fastest.
Arguments:
- hidden_in: bfloat16 [256, 2048], P(None, 'head'), may hold values from -1.5 to 1.5
- attention_gain: float32 [2048], replicated, may hold values from 0.1 to 1.9
- query_gain: float32 [64], replicated, may hold values from 0.5 to 2
- key_gain: float32 [64], replicated, may hold values from 1.5 to 4
- feedforward_gain: float32 [2048], replicated, may hold values from 0.1 to 1.9
- input_weight: bfloat16 [2048, 1920], P('req', 'head'), may hold values from -0.125 to 0.125
- output_weight: bfloat16 [1280, 2048], P('req', 'head'), may hold values from -0.15625 to 0.15625
- gate_weight: bfloat16 [2048, 5120], P('req', 'head'), may hold values from -0.125 to 0.125
- up_weight: bfloat16 [2048, 5120], P('req', 'head'), may hold values from -0.125 to 0.125
- down_weight: bfloat16 [5120, 2048], P('req', 'head'), may hold values from -0.078125 to 0.078125
- old_cache: bfloat16 [4096, 128, 640], P(('req', 'head')), may hold values from -400 to 400
- keep_rows: int32 [4096, 64], P(('req', 'head')), may hold values from -1 to 127, as said below
- drop_weights: float32 [4096, 128], P(('req', 'head')), may hold values from 0.1 to 1
- dest_slots: int32 [512, 8], P(('req', 'head')), may hold values from 0 to 7, each once within a row
- lengths: int32 [256], replicated, may hold values from 1 to 16, 2048 in all
- page_table: int32 [256, 16], P('req'), may hold values from 0 to 7, as said below
- source: int32 [128], replicated, may hold values from 0 to 127, each once
Outputs:
- compact_cache: bfloat16 [2048, 128, 640], P(('req', 'head'))
- summary_rows: bfloat16 [4096, 640], P(('req', 'head'))
- hidden_out: bfloat16 [256, 2048], P(None, 'head')
Inputs may be any that keep to these rules, and one draw needn't show every extreme that they name: `keep_rows`: row p lists kept rows of page p in ascending order, from 32 to 64 of them, then -1 to the end; some page keeps 64. `page_table`: row g * 2 + k belongs to the k-th request held by index g of req; entry j is the slot, on the device with req index g and head index j % 4, of that request's j-th page. On every device the entries that point to it form a permutation of its 8 slots. `source`: A permutation of the continued requests over the held slots. `dest_slots`: each row is a permutation. `lengths`: they sum to 2048 and the largest is 16.
All inputs are finite; a program needn't handle non-finite values.
Results may differ from a plain program's by a relative error of at most 0.015.
The roundings to bfloat16 on the way count: a program that leaves them out, or rounds other values in their place, can miss the bound.
Values may be sent and summed in bfloat16 or wider, within the bound.
A program may use at most 64 MiB of HBM per device.

v0:
```python
import jax
import jax.numpy as jnp
from jax import lax
from jax.sharding import PartitionSpec as P

D = 2048
HEADS = 20
KVH = 5
HD = 64
FF = 5120
PAGE = 128
KEEP = 64
NP = 16
R_DEV = 2
KVW = 640
epsilon = 1e-06
negative = -1e30


def joined(part, axis, combine):
    gathered = jax.tree.map(lambda a: lax.all_gather(a, axis), part)

    def take(source):
        return jax.tree.map(lambda a: lax.dynamic_index_in_dim(a, source, 0, False), gathered)

    return lax.fori_loop(
        1, lax.axis_size(axis), lambda source, state: combine(state, take(source)), take(0)
    )


def rms_rows(values, gain):
    mean_square = jnp.mean(values * values, axis=-1, keepdims=True)
    return values * lax.rsqrt(mean_square + epsilon) * gain


def rotate(vectors, positions):
    half = vectors.shape[-1] // 2
    frequency = 10000.0 ** (-jnp.arange(half, dtype=jnp.float32) / half)
    angles = positions.astype(jnp.float32)[:, None] * frequency[None, :]
    cosine = jnp.cos(angles)[:, None, :]
    sine = jnp.sin(angles)[:, None, :]
    first = vectors[..., :half]
    second = vectors[..., half:]
    return jnp.concatenate(
        [first * cosine - second * sine, second * cosine + first * sine], axis=-1
    )


def compact_pages(pages, keep, weights):
    rows = jnp.arange(pages.shape[1], dtype=jnp.int32)
    picks = keep[:, :, None] == rows[None, None, :]
    kept = jnp.einsum(
        "pkr,prc->pkc", picks.astype(jnp.bfloat16), pages, preferred_element_type=jnp.float32
    ).astype(jnp.bfloat16)
    dropped = weights * (1.0 - jnp.sum(picks.astype(jnp.float32), axis=1))
    total = jnp.sum(dropped, axis=1)
    means = (
        jnp.einsum(
            "pr,prc->pc", dropped, pages.astype(jnp.float32), precision=lax.Precision.HIGHEST
        )
        / total[:, None]
    )
    return (kept, means.astype(jnp.bfloat16), jnp.log(total))


def merge_parts(first, second):
    top_first, mass_first, sum_first = first
    top_second, mass_second, sum_second = second
    top = jnp.maximum(top_first, top_second)
    scale_first = jnp.exp(top_first - top)
    scale_second = jnp.exp(top_second - top)
    mass = mass_first * scale_first + mass_second * scale_second
    summed = sum_first * scale_first[..., None] + sum_second * scale_second[..., None]
    return (top, mass, summed)


def held_request(rows, source):
    half = R_DEV // 2
    position = rows % R_DEV
    slot = rows // R_DEV * half + position - half
    continued = jnp.arange(source.shape[0], dtype=jnp.int32)
    matches = source[None, :] == slot[:, None]
    owner_cont = jnp.sum(jnp.where(matches, continued[None, :], 0), axis=1)
    carried = owner_cont // half * R_DEV + half + owner_cont % half
    return jnp.where(position < half, rows, carried)


def full_rows(values):
    return lax.all_gather(values, "head", axis=1, tiled=True)


def feature_block(rows, count):
    return lax.dynamic_slice_in_dim(rows, lax.axis_index("req") * count, count, 1)


def normed_block(rows, gain, count):
    whole = full_rows(rows)
    normed = rms_rows(whole.astype(jnp.float32), gain).astype(jnp.bfloat16)
    return feature_block(normed, count)


def input_block(rows, count):
    return feature_block(full_rows(rows), count)


def project(inputs, weight):
    return lax.psum(jnp.dot(inputs, weight, preferred_element_type=jnp.float32), "req")


def on_device(
    hidden_in,
    attention_gain,
    query_gain,
    key_gain,
    feedforward_gain,
    input_weight,
    output_weight,
    gate_weight,
    up_weight,
    down_weight,
    old_cache,
    keep_rows,
    drop_weights,
    dest_slots,
    lengths,
    page_table,
    source,
):
    groups = lax.axis_size("req")
    lanes = lax.axis_size("head")
    group = lax.axis_index("req")
    lane = lax.axis_index("head")
    requests = hidden_in.shape[0]
    half = R_DEV // 2
    split = KVH * HD
    ratio = HEADS // KVH
    scale = HD ** (-0.5)
    pages_here = old_cache.shape[0]
    slots = jnp.arange(R_DEV, dtype=jnp.int32)
    held = held_request(group * R_DEV + slots, source)
    held_len = lengths[held]
    positions = held_len * PAGE
    inputs = normed_block(hidden_in, attention_gain, D // groups)
    partial_qkv = jnp.dot(inputs, input_weight, preferred_element_type=jnp.float32)
    mixed = lax.psum(partial_qkv, "req").astype(jnp.bfloat16)
    qkv = lax.all_gather(mixed, "head", axis=1, tiled=True)
    held_qkv = qkv[held].astype(jnp.float32)
    query = rotate(
        rms_rows(held_qkv[:, : HEADS * HD].reshape(R_DEV, HEADS, HD), query_gain), positions
    ).astype(jnp.bfloat16)
    key_new = rotate(
        rms_rows(held_qkv[:, HEADS * HD : (HEADS + KVH) * HD].reshape(R_DEV, KVH, HD), key_gain),
        positions,
    ).astype(jnp.bfloat16)
    value_new = held_qkv[:, (HEADS + KVH) * HD :].reshape(R_DEV, KVH, HD)
    kept, means, bias = compact_pages(old_cache, keep_rows, drop_weights)
    destination = dest_slots[0]
    fresh_ids = jnp.arange(pages_here, dtype=jnp.int32)
    inverse = jnp.sum(
        jnp.where(destination[None, :] == fresh_ids[:, None], fresh_ids[None, :], 0), axis=1
    )
    compact = kept[inverse].reshape(pages_here // 2, PAGE, KVW)
    summaries = means[inverse]
    per_lane = NP // lanes
    table = page_table.reshape(R_DEV, per_lane, lanes)
    mine = lax.dynamic_slice_in_dim(table, lane, 1, 2)[:, :, 0]
    logical = jnp.arange(per_lane, dtype=jnp.int32) * lanes + lane
    live = logical[None, :] < held_len[:, None]
    owner = jnp.any((mine[:, :, None] == fresh_ids[None, None, :]) & live[:, :, None], axis=1)
    query_groups = query.reshape(R_DEV, KVH, ratio, HD)
    row_keys = kept[:, :, :split].reshape(pages_here, KEEP, KVH, HD)
    row_values = kept[:, :, split:].reshape(pages_here, KEEP, KVH, HD)
    row_live = keep_rows >= 0
    allowed = owner[:, None, None, :, None] & row_live[None, None, None, :, :]
    scores = (
        jnp.einsum("rngd,pmnd->rngpm", query_groups, row_keys, preferred_element_type=jnp.float32)
        * scale
    )
    scores = jnp.where(allowed, scores, negative)
    mean_keys = means[:, :split].reshape(pages_here, KVH, HD)
    mean_values = means[:, split:].reshape(pages_here, KVH, HD)
    mean_scores = (
        jnp.einsum("rngd,pnd->rngp", query_groups, mean_keys, preferred_element_type=jnp.float32)
        * scale
        + bias[None, None, None, :]
    )
    mean_allowed = owner[:, None, None, :]
    mean_scores = jnp.where(mean_allowed, mean_scores, negative)
    top = jnp.maximum(jnp.max(scores, axis=(3, 4)), jnp.max(mean_scores, axis=3))
    row_weight = jnp.where(allowed, jnp.exp(scores - top[..., None, None]), 0.0)
    mean_weight = jnp.where(mean_allowed, jnp.exp(mean_scores - top[..., None]), 0.0)
    mass = jnp.sum(row_weight, axis=(3, 4)) + jnp.sum(mean_weight, axis=3)
    total = jnp.einsum(
        "rngpm,pmnd->rngd",
        row_weight,
        row_values.astype(jnp.float32),
        precision=lax.Precision.HIGHEST,
    )
    total = total + jnp.einsum(
        "rngp,pnd->rngd",
        mean_weight,
        mean_values.astype(jnp.float32),
        precision=lax.Precision.HIGHEST,
    )
    top, mass, total = joined((top, mass, total), "head", merge_parts)
    own_score = (
        jnp.einsum("rngd,rnd->rng", query_groups, key_new, preferred_element_type=jnp.float32)
        * scale
    )
    final_top = jnp.maximum(top, own_score)
    earlier = jnp.exp(top - final_top)
    own_weight = jnp.exp(own_score - final_top)
    mass = mass * earlier + own_weight
    total = total * earlier[..., None] + own_weight[..., None] * value_new[:, :, None, :]
    attention = (total / mass[..., None]).reshape(R_DEV, HEADS * HD).astype(jnp.bfloat16)
    moved = lax.all_to_all(attention, "req", split_axis=1, concat_axis=0, tiled=True)
    everyone = jnp.arange(requests, dtype=jnp.int32)
    position = everyone % R_DEV
    cont_index = everyone // R_DEV * half + position - half
    slot_of = source[jnp.clip(cont_index, 0, source.shape[0] - 1)]
    held_row = slot_of // half * R_DEV + half + slot_of % half
    row_of = jnp.where(position < half, everyone, held_row)
    attention_rows = moved[row_of]
    projected = project(attention_rows, output_weight)
    mid = (hidden_in.astype(jnp.float32) + projected).astype(jnp.bfloat16)
    inputs_mid = normed_block(mid, feedforward_gain, D // groups)
    both = jnp.concatenate([gate_weight, up_weight], axis=1)
    local_units = gate_weight.shape[1]
    sums = lax.psum(jnp.dot(inputs_mid, both, preferred_element_type=jnp.float32), "req")
    active = (jax.nn.silu(sums[:, :local_units]) * sums[:, local_units:]).astype(jnp.bfloat16)
    down = project(input_block(active, FF // groups), down_weight)
    residual = lax.optimization_barrier(mid).astype(jnp.float32)
    result = (residual + down).astype(jnp.bfloat16)
    return (compact, summaries, result)


def solution(mesh):
    placed = (
        P(None, "head"),
        P(),
        P(),
        P(),
        P(),
        P("req", "head"),
        P("req", "head"),
        P("req", "head"),
        P("req", "head"),
        P("req", "head"),
        P(("req", "head"), None, None),
        P(("req", "head"), None),
        P(("req", "head"), None),
        P(("req", "head"), None),
        P(),
        P("req", None),
        P(),
    )
    return jax.shard_map(
        on_device,
        mesh=mesh,
        in_specs=placed,
        out_specs=(P(("req", "head"), None, None), P(("req", "head"), None), P(None, "head")),
        check_vma=False,
    )
```

profile of v0, /device:TPU:24, one launch (start us, length us, event | category | flops | bytes accessed | tf_op | source)
XLA Modules:
  0.0 1286.6 jit_solution(14385195051736186096)
XLA Ops:
  7.2 0.7 all-gather.7.cloned.1.call-update
  8.0 0.8 fusion.49
  8.8 1.9 gather_fusion.4
  10.7 0.8 reshape.428
  11.5 1.3 gather_fusion.2
  12.9 0.2 dynamic-slice_reduce_fusion
  13.3 0.8 convert_reduce_fusion
  14.2 0.8 fusion.64
  15.0 1.1 convolution_convert_fusion
  16.1 0.7 fusion.70
  16.9 0.2 fusion.65
  17.3 1.1 copy.94
  18.5 1.1 copy.84
  19.6 0.8 dynamic-slice
  20.4 0.1 multiply_cosine_fusion
  20.6 23.2 %all-gather.7.cloned.1.call-done = bf16[256,2048]{1,0:T(8,128)(2,1)} async-done(((bf16[256,512]{1,0:T(8,128)(2,1)}), bf16[256,2048]{1,0:T(8,128)(2,1)}) %all-gather.7.cloned.1.call-update) | async-done | bytes 1048592 | tf_op jit(solution)/shard_map/all_gather | solution.py:89
  43.8 1.5 multiply_reduce_fusion.1
  45.3 1.5 convert_element_type.68
  46.8 0.4 fusion.23
  47.2 480.6 %all-reduce.10 = bf16[256,480]{0,1:T(8,128)(2,1)S(1)} all-reduce(f32[256,480]{0,1:T(8,128)S(1)} %fusion.23), channel_id=1, replica_groups=mesh['req'=128,'head'=4] {'req'}, use_global_device_ids=true, to_apply=%region_6.7 | all-reduce | flops 122880 | bytes 737280 | tf_op jit(solution)/shard_map/psum | solution.py:145
  527.8 14.1 %all_gather.27 = bf16[256,1920]{0,1:T(8,128)(2,1)S(1)} all-gather(bf16[256,480]{0,1:T(8,128)(2,1)S(1)} %all-reduce.10), channel_id=1, replica_groups=mesh['req'=128,'head'=4] {'head'}, dimensions={1}, use_global_device_ids=true | all-gather | bytes 1228800 | tf_op jit(solution)/shard_map/all_gather | solution.py:146
  542.0 1.4 copy.85
  543.4 2.0 gather_fusion.3
  546.4 0.1 fusion.40
  546.5 0.1 copy.114
  546.6 1.4 fusion.68
  548.0 0.2 fusion.69
  548.2 0.1 copy.92
  548.3 0.2 fusion.63
  548.6 0.2 fusion.34
  548.8 0.1 copy.93
  548.9 11.9 all-gather.1
  560.8 11.9 all-gather
  572.7 0.6 convolution_bitcast_fusion
  573.3 0.2 fusion.7
  573.6 11.9 all-gather.2
  585.5 1.1 while.19
  585.7 0.1 fusion.83
  586.1 0.1 fusion.83
  586.4 0.1 fusion.83
  586.6 0.1 copy.102
  586.9 0.1 fusion.33
  587.0 0.2 convert_element_type.74
  587.1 0.7 copy.103
  587.8 21.1 %all-to-all-start = ((bf16[2,128,10]{2,0,1:T(2,128)(2,1)}), bf16[2,128,10]{2,0,1:T(2,128)(2,1)S(1)}, u32[]{:S(2)}, u32[]{:S(2)}) async-start(bf16[2,128,10]{2,0,1:T(2,128)(2,1)} %copy.103), calls=%async_computation | async-start | bytes 131072 | tf_op jit(solution)/shard_map/all_to_all | solution.py:216
  609.0 9.2 all-to-all-done
  618.2 0.9 gather_fusion.5
  619.1 1.0 fusion.71
  620.2 185.8 %all-reduce.5.cloned.1.call-done = f32[256,512]{1,0:T(8,128)} async-done(((f32[256,512]{1,0:T(8,128)}), f32[256,512]{1,0:T(8,128)}) %all-reduce.5.cloned.1.call-update) | async-done | bytes 524304 | tf_op jit(solution)/shard_map/psum | solution.py:107
  805.9 1.8 add_convert_fusion.1
  807.8 0.8 dynamic-slice.1
  808.6 25.2 %all-gather.9.cloned.1.call-done = bf16[256,2048]{1,0:T(8,128)(2,1)} async-done(((bf16[256,512]{1,0:T(8,128)(2,1)}), bf16[256,2048]{1,0:T(8,128)(2,1)}) %all-gather.9.cloned.1.call-update) | async-done | bytes 1048592 | tf_op jit(solution)/shard_map/all_gather | solution.py:89
  833.8 1.5 multiply_reduce_fusion
  835.4 1.5 convert_element_type.77
  836.8 2.1 fusion.19
  839.0 203.2 %all-reduce.7.cloned.1.call-done = f32[256,2560]{1,0:T(8,128)} async-done(((f32[256,2560]{1,0:T(8,128)}), f32[256,2560]{1,0:T(8,128)}) %all-reduce.7.cloned.1.call-update) | async-done | bytes 2621456 | tf_op jit(solution)/shard_map/psum | solution.py:229
  1042.2 2.9 fusion.4
  1045.2 0.1 select_reduce_fusion
  1045.3 36.2 %all-gather.11.cloned.1.call-done = bf16[256,5120]{1,0:T(8,128)(2,1)} async-done(((bf16[256,1280]{1,0:T(8,128)(2,1)}), bf16[256,5120]{1,0:T(8,128)(2,1)}) %all-gather.11.cloned.1.call-update) | async-done | bytes 2621456 | tf_op jit(solution)/shard_map/all_gather | solution.py:89
  1081.6 2.0 fusion.30
  1083.6 1.2 gather_fusion.1
  1084.8 1.5 gather_fusion
  1086.3 191.7 %all-reduce.9.cloned.1.call-done = f32[256,512]{1,0:T(8,128)} async-done(((f32[256,512]{1,0:T(8,128)}), f32[256,512]{1,0:T(8,128)}) %all-reduce.9.cloned.1.call-update) | async-done | bytes 524304 | tf_op jit(solution)/shard_map/psum | solution.py:107
  1278.0 1.8 add_convert_fusion
  (99 shorter events, 3.1 us)
Async XLA Ops:
  7.2 7.8 copy-start
  7.2 36.6 %all-gather.7.cloned.1.call-start = ((), (), s32[]{:S(2)}) async-start(), calls=%async_computation.1 | async-start | bytes 1310720 | tf_op jit(solution)/shard_map/all_gather | solution.py:89
  16.8 3.7 copy-start.7
  20.6 26.2 %copy-start.8 = (bf16[16,480]{1,0:T(8,128)(2,1)S(1)}, bf16[16,480]{1,0:T(8,128)(2,1)}, u32[]{:S(2)}) copy-start(bf16[16,480]{1,0:T(8,128)(2,1)} %param.24) | copy-start | bytes 46084
  47.2 498.6 %copy-start.11 = (f32[64]{0:T(128)S(1)}, f32[64]{0:T(128)}, u32[]{:S(2)}) copy-start(f32[64]{0:T(128)} %param.22) | copy-start | bytes 772
  47.2 498.7 %copy-start.10 = (f32[64]{0:T(128)S(1)}, f32[64]{0:T(128)}, u32[]{:S(2)}) copy-start(f32[64]{0:T(128)} %param.21) | copy-start | bytes 772
  543.4 29.3 %copy-start.3 = (bf16[8,64,320]{1,2,0:T(8,128)(2,1)S(1)}, bf16[8,64,320]{1,2,0:T(8,128)(2,1)}, u32[]{:S(2)}) copy-start(bf16[8,64,320]{1,2,0:T(8,128)(2,1)} %copy.94) | copy-start | bytes 983044
  548.0 71.1 %copy-start.9 = (bf16[10,512]{1,0:T(8,128)(2,1)S(1)}, bf16[10,512]{1,0:T(8,128)(2,1)}, u32[]{:S(2)}) copy-start(bf16[10,512]{1,0:T(8,128)(2,1)} %param.25) | copy-start | bytes 30724
  572.7 233.2 %copy-start.2 = (bf16[256,512]{1,0:T(8,128)(2,1)S(1)}, bf16[256,512]{1,0:T(8,128)(2,1)}, u32[]{:S(2)}) copy-start(bf16[256,512]{1,0:T(8,128)(2,1)} %param.19) | copy-start | bytes 786436
  587.8 30.4 %all-to-all-start = ((bf16[2,128,10]{2,0,1:T(2,128)(2,1)}), bf16[2,128,10]{2,0,1:T(2,128)(2,1)S(1)}, u32[]{:S(2)}, u32[]{:S(2)}) async-start(bf16[2,128,10]{2,0,1:T(2,128)(2,1)} %copy.103), calls=%async_computation | async-start | bytes 131072 | tf_op jit(solution)/shard_map/all_to_all | solution.py:216
  608.9 197.0 %all-reduce.5.cloned.1.call-start = ((), (), s32[]{:S(2)}) async-start(), calls=%async_computation.2 | async-start | bytes 1048576 | tf_op jit(solution)/shard_map/psum | solution.py:107
  620.1 213.7 %all-gather.9.cloned.1.call-start = ((), (), s32[]{:S(2)}) async-start(), calls=%async_computation.3 | async-start | bytes 1310720 | tf_op jit(solution)/shard_map/all_gather | solution.py:89
  807.8 234.5 %all-reduce.7.cloned.1.call-start = ((), (), s32[]{:S(2)}) async-start(), calls=%async_computation.4 | async-start | bytes 5242880 | tf_op jit(solution)/shard_map/psum | solution.py:229
  808.6 28.2 %copy-start.5 = (bf16[16,1280]{1,0:T(8,128)(2,1)S(1)}, bf16[16,1280]{1,0:T(8,128)(2,1)}, u32[]{:S(2)}) copy-start(bf16[16,1280]{1,0:T(8,128)(2,1)} %param.27) | copy-start | bytes 122884
  808.6 28.2 %copy-start.6 = (bf16[16,1280]{1,0:T(8,128)(2,1)S(1)}, bf16[16,1280]{1,0:T(8,128)(2,1)}, u32[]{:S(2)}) copy-start(bf16[16,1280]{1,0:T(8,128)(2,1)} %param.26) | copy-start | bytes 122884
  839.0 206.3 %copy-start.12 = (s32[1,8]{1,0:T(1,128)S(1)}, s32[1,8]{1,0:T(1,128)}, u32[]{:S(2)}) copy-start(s32[1,8]{1,0:T(1,128)} %param.32) | copy-start | bytes 100
  839.0 242.6 %copy-start.4 = (bf16[40,512]{1,0:T(8,128)(2,1)S(1)}, bf16[40,512]{1,0:T(8,128)(2,1)}, u32[]{:S(2)}) copy-start(bf16[40,512]{1,0:T(8,128)(2,1)} %param.28) | copy-start | bytes 122884
  839.0 242.6 %all-gather.11.cloned.1.call-start = ((), (), s32[]{:S(2)}) async-start(), calls=%async_computation.5 | async-start | bytes 3276800 | tf_op jit(solution)/shard_map/all_gather | solution.py:89
  1045.1 232.8 %copy-start.1 = (bf16[256,512]{1,0:T(8,128)(2,1)S(1)}, bf16[256,512]{1,0:T(8,128)(2,1)}, u32[]{:S(2)}) copy-start(bf16[256,512]{1,0:T(8,128)(2,1)} %add_convert_fusion.1) | copy-start | bytes 786436
  1045.2 232.8 %all-reduce.9.cloned.1.call-start = ((), (), s32[]{:S(2)}) async-start(), calls=%async_computation.6 | async-start | bytes 1048576 | tf_op jit(solution)/shard_map/psum | solution.py:107
Sparse Core Ops, SparseCore 0:
  10.1 33.6 all-gather.6
  620.2 185.6 all-reduce.4
  808.6 25.1 all-gather.8
  839.1 203.0 all-reduce.6
  1045.3 36.2 all-gather.10
  1085.0 192.9 all-reduce.8
where the time goes:
time: 1290 us
  waiting for transfers between devices  675 us (52%)
  blocking collectives  530 us (41%)
  starting transfers between devices  21.3 us (2%)
  local copies, waits for them, and re-layouts  17.8 us (1%)
  other arithmetic  17.2 us (1%)
  between operations  14.5 us (1%)
    psum x1, blocking collectives, on_device(): mixed = lax.psum(partial_qkv, 'req').astype(jnp.bfloat16)  481 us
    psum x2, waiting for transfers between devices, project(): lax.psum(jnp.dot(inputs, weight, preferred_element_type=jnp.float32), 'req')  378 us
    psum x1, waiting for transfers between devices, on_device(): lax.psum(jnp.dot(inputs_mid, both, preferred_element_type=jnp.float32), '...  203 us
    all_gather x3, waiting for transfers between devices, full_rows(): return lax.all_gather(values, 'head', axis=1, tiled=True)  84.7 us
    all_gather x3, blocking collectives, joined(): gathered = jax.tree.map(lambda a: lax.all_gather(a, axis), part)  35.7 us
  transfers between devices with their start and end apart: 7, of which 7 were waited for; matrix products, arithmetic and copies ran while one was open for 1% of the time, Pallas kernels for 0%

commit v1 on v0

--- a/solution.py
+++ b/solution.py
@@ -15,6 +15,27 @@
 KVW = 640
 epsilon = 1e-06
 negative = -1e30
+
+
+def gather_around(x, axis, dim):
+    peers, index, rows = (lax.axis_size(axis), lax.axis_index(axis), x.shape[dim])
+    ahead = [(i, (i + 1) % peers) for i in range(peers)]
+    left = [(i, (i - 1) % peers) for i in range(peers)]
+    out = jnp.zeros((*x.shape[:dim], peers * rows, *x.shape[dim + 1 :]), x.dtype)
+    out = lax.dynamic_update_slice_in_dim(out, x, index * rows, axis=dim)
+    from_left = from_right = x
+    half = peers // 2
+    for step in range(1, half + 1):
+        from_left = lax.ppermute(from_left, axis, ahead)
+        out = lax.dynamic_update_slice_in_dim(
+            out, from_left, (index - step) % peers * rows, axis=dim
+        )
+        if step < peers - half:
+            from_right = lax.ppermute(from_right, axis, left)
+            out = lax.dynamic_update_slice_in_dim(
+                out, from_right, (index + step) % peers * rows, axis=dim
+            )
+    return out
 
 
 def joined(part, axis, combine):
@@ -86,7 +107,7 @@
 
 
 def full_rows(values):
-    return lax.all_gather(values, "head", axis=1, tiled=True)
+    return gather_around(values, "head", 1)
 
 
 def feature_block(rows, count):

time: 1290 us -> 1270 us (0.984)
  waiting for transfers between devices: 675 us -> 614 us
  starting transfers between devices: 21.3 us -> 49 us
  local copies, waits for them, and re-layouts: 17.8 us -> 31.8 us
    all_gather x3 -> x0, waiting for transfers between devices: 84.7 us -> none  [full_rows(): return lax.all_gather(values, 'head', axis=1, tiled=True)]
    ppermute x0 -> x9, waiting for transfers between devices: none -> 34.5 us  [the longest x6 34.5 us: gather_around(): from_left = lax.ppermute(from_left, axis, ahead)]
    ppermute x0 -> x9, starting transfers between devices: none -> 27.8 us  [the longest x6 15.7 us: gather_around(): from_left = lax.ppermute(from_left, axis, ahead)]
  transfers between devices with their start and end apart: 7 -> 13, of which waited for: 7 -> 9; matrix products, arithmetic and copies ran while one was open for 1% -> 2% of each run, Pallas kernels for 0% -> 0%
where the time goes in v1:
time: 1270 us
  waiting for transfers between devices  614 us (48%)
  blocking collectives  536 us (42%)
  starting transfers between devices  49 us (4%)
  local copies, waits for them, and re-layouts  31.8 us (3%)
  between operations  14.4 us (1%)
    psum x1, blocking collectives, on_device(): mixed = lax.psum(partial_qkv, 'req').astype(jnp.bfloat16)  486 us
    psum x2, waiting for transfers between devices, project(): lax.psum(jnp.dot(inputs, weight, preferred_element_type=jnp.float32), 'req')  372 us
    psum x1, waiting for transfers between devices, on_device(): lax.psum(jnp.dot(inputs_mid, both, preferred_element_type=jnp.float32), '...  199 us
    all_gather x3, blocking collectives, joined(): gathered = jax.tree.map(lambda a: lax.all_gather(a, axis), part)  35.7 us
    ppermute x6, waiting for transfers between devices, gather_around(): from_left = lax.ppermute(from_left, axis, ahead)  34.5 us
  transfers between devices with their start and end apart: 13, of which 9 were waited for; matrix products, arithmetic and copies ran while one was open for 2% of the time, Pallas kernels for 0%

profile of v1, /device:TPU:24, one launch (start us, length us, event | category | flops | bytes accessed | tf_op | source)
XLA Modules:
  0.0 1265.9 jit_solution(17888050639050232173)
XLA Ops:
  7.2 4.8 collective-permute-start.1
  12.0 1.9 collective-permute-start
  14.0 0.7 broadcast_compare_fusion
  14.7 0.8 convert_reduce_fusion
  15.5 0.8 fusion.52
  16.4 1.9 gather_fusion.4
  18.3 1.3 gather_fusion.2
  19.7 0.8 reshape.428
  20.9 1.1 convolution_convert_fusion
  22.1 0.7 fusion.71
  23.0 1.0 fusion.66
  24.2 2.7 collective-permute-start.2
  27.0 1.0 constant_dynamic-update-slice_fusion.11
  28.2 2.1 copy.94
  30.3 1.1 copy.84
  31.4 0.8 dynamic-slice
  32.2 1.0 constant_dynamic-update-slice_fusion.10
  33.2 1.0 constant_dynamic-update-slice_fusion.9
  34.1 1.2 collective-permute-done.2
  35.4 1.0 constant_dynamic-update-slice_fusion.8
  37.1 0.4 fusion.23
  37.5 485.8 %all-reduce.10 = bf16[256,480]{0,1:T(8,128)(2,1)S(1)} all-reduce(f32[256,480]{0,1:T(8,128)S(1)} %fusion.23), channel_id=1, replica_groups=mesh['req'=128,'head'=4] {'req'}, use_global_device_ids=true, to_apply=%region_6.7 | all-reduce | flops 122880 | bytes 737280 | tf_op jit(solution)/shard_map/psum | solution.py:166
  523.2 14.5 %all_gather.17 = bf16[256,1920]{0,1:T(8,128)(2,1)S(1)} all-gather(bf16[256,480]{0,1:T(8,128)(2,1)S(1)} %all-reduce.10), channel_id=1, replica_groups=mesh['req'=128,'head'=4] {'head'}, dimensions={1}, use_global_device_ids=true | all-gather | bytes 1228800 | tf_op jit(solution)/shard_map/all_gather | solution.py:167
  537.8 1.4 copy.85
  539.2 2.0 gather_fusion.3
  542.5 1.4 fusion.69
  544.7 11.9 all-gather.1
  556.6 11.9 all-gather
  568.5 0.6 convolution_bitcast_fusion
  569.4 11.9 all-gather.2
  581.3 1.1 while.19
  583.0 0.7 copy.103
  583.7 21.0 %all-to-all-start = ((bf16[2,128,10]{2,0,1:T(2,128)(2,1)}), bf16[2,128,10]{2,0,1:T(2,128)(2,1)S(1)}, u32[]{:S(2)}, u32[]{:S(2)}) async-start(bf16[2,128,10]{2,0,1:T(2,128)(2,1)} %copy.103), calls=%async_computation | async-start | bytes 131072 | tf_op jit(solution)/shard_map/all_to_all | solution.py:237
  604.8 9.2 all-to-all-done
  614.0 0.9 gather_fusion.5
  614.9 1.0 fusion.72
  615.9 185.7 %all-reduce.5.cloned.1.call-done = f32[256,512]{1,0:T(8,128)} async-done(((f32[256,512]{1,0:T(8,128)}), f32[256,512]{1,0:T(8,128)}) %all-reduce.5.cloned.1.call-update) | async-done | bytes 524304 | tf_op jit(solution)/shard_map/psum | solution.py:128
  801.7 1.1 constant_dynamic-update-slice_fusion.7
  802.9 3.4 collective-permute-start.3
  806.2 3.7 collective-permute-start.4
  809.9 3.4 collective-permute-done.3
  813.3 2.2 collective-permute-start.5
  815.5 0.8 dynamic-slice.1
  816.3 6.5 collective-permute-done.5
  822.9 0.3 multiply_reduce_fusion
  823.6 2.1 fusion.19
  825.8 198.6 %all-reduce.7.cloned.1.call-done = f32[256,2560]{1,0:T(8,128)} async-done(((f32[256,2560]{1,0:T(8,128)}), f32[256,2560]{1,0:T(8,128)}) %all-reduce.7.cloned.1.call-update) | async-done | bytes 2621456 | tf_op jit(solution)/shard_map/psum | solution.py:250
  1024.4 1.8 broadcast_in_dim.78
  1026.2 0.9 copy-done.1
  1027.1 1.3 constant_dynamic-update-slice_fusion.3
  1028.4 3.4 collective-permute-start.6
  1031.7 3.7 collective-permute-start.7
  1035.4 11.5 collective-permute-done.6
  1046.9 2.2 collective-permute-start.8
  1049.1 0.6 select_reduce_fusion
  1049.7 0.9 constant_dynamic-update-slice_fusion.2
  1050.7 2.0 constant_dynamic-update-slice_fusion.1
  1052.7 11.9 collective-permute-done.8
  1064.6 2.0 constant_dynamic-update-slice_fusion
  1066.6 2.0 fusion.30
  1068.6 1.2 gather_fusion.1
  1069.8 1.5 gather_fusion
  1071.3 186.3 %all-reduce.9.cloned.1.call-done = f32[256,512]{1,0:T(8,128)} async-done(((f32[256,512]{1,0:T(8,128)}), f32[256,512]{1,0:T(8,128)}) %all-reduce.9.cloned.1.call-update) | async-done | bytes 524304 | tf_op jit(solution)/shard_map/psum | solution.py:128
  1257.6 1.8 add_convert_fusion
  (123 shorter events, 6.8 us)
Async XLA Ops:
  7.2 13.7 %copy-start = (bf16[8,128,640]{2,1,0:T(8,128)(2,1)S(1)}, bf16[8,128,640]{2,1,0:T(8,128)(2,1)}, u32[]{:S(2)}) copy-start(bf16[8,128,640]{2,1,0:T(8,128)(2,1)} %param.29) | copy-start | bytes 3932164
  7.2 14.8 %copy-start.9 = (f32[8,128]{1,0:T(8,128)S(1)}, f32[8,128]{1,0:T(8,128)}, u32[]{:S(2)}) copy-start(f32[8,128]{1,0:T(8,128)} %param.31) | copy-start | bytes 12292
  7.2 26.0 %collective-permute-start.1 = (bf16[256,512]{1,0:T(8,128)(2,1)}, bf16[256,512]{1,0:T(8,128)(2,1)}, u32[]{:S(2)}, u32[]{:S(2)}) collective-permute-start(bf16[256,512]{1,0:T(8,128)(2,1)} %param.19), channel_id=1, source_target_pairs={{0,3},{1,0},{2,1},{3,2},{4,7},{5,4},{6,5},{7,6},{8,11},{9,8},{10,9... | collective-permute-start | bytes 786440 | tf_op jit(solution)/shard_map/ppermute | solution.py:34
  12.0 12.2 collective-permute-start
  24.2 11.2 collective-permute-start.2
  36.3 0.7 copy-start.7
  37.5 504.2 %copy-start.11 = (f32[64]{0:T(128)S(1)}, f32[64]{0:T(128)}, u32[]{:S(2)}) copy-start(f32[64]{0:T(128)} %param.22) | copy-start | bytes 772
  37.5 504.3 %copy-start.10 = (f32[64]{0:T(128)S(1)}, f32[64]{0:T(128)}, u32[]{:S(2)}) copy-start(f32[64]{0:T(128)} %param.21) | copy-start | bytes 772
  539.2 29.3 %copy-start.3 = (bf16[8,64,320]{1,2,0:T(8,128)(2,1)S(1)}, bf16[8,64,320]{1,2,0:T(8,128)(2,1)}, u32[]{:S(2)}) copy-start(bf16[8,64,320]{1,2,0:T(8,128)(2,1)} %copy.94) | copy-start | bytes 983044
  543.8 71.0 %copy-start.8 = (bf16[10,512]{1,0:T(8,128)(2,1)S(1)}, bf16[10,512]{1,0:T(8,128)(2,1)}, u32[]{:S(2)}) copy-start(bf16[10,512]{1,0:T(8,128)(2,1)} %param.25) | copy-start | bytes 30724
  581.3 220.4 %copy-start.2 = (bf16[256,512]{1,0:T(8,128)(2,1)S(1)}, bf16[256,512]{1,0:T(8,128)(2,1)}, u32[]{:S(2)}) copy-start(bf16[256,512]{1,0:T(8,128)(2,1)} %param.19) | copy-start | bytes 786436
  583.7 30.3 %all-to-all-start = ((bf16[2,128,10]{2,0,1:T(2,128)(2,1)}), bf16[2,128,10]{2,0,1:T(2,128)(2,1)S(1)}, u32[]{:S(2)}, u32[]{:S(2)}) async-start(bf16[2,128,10]{2,0,1:T(2,128)(2,1)} %copy.103), calls=%async_computation | async-start | bytes 131072 | tf_op jit(solution)/shard_map/all_to_all | solution.py:237
  604.7 196.9 %all-reduce.5.cloned.1.call-start = ((), (), s32[]{:S(2)}) async-start(), calls=%async_computation.1 | async-start | bytes 1048576 | tf_op jit(solution)/shard_map/psum | solution.py:128
  615.9 408.5 %all-reduce.7.cloned.1.call-start = ((), (), s32[]{:S(2)}) async-start(), calls=%async_computation.2 | async-start | bytes 5242880 | tf_op jit(solution)/shard_map/psum | solution.py:250
  802.9 10.4 collective-permute-start.3
  806.2 10.0 collective-permute-start.4
  813.3 9.5 collective-permute-start.5
  822.8 0.8 copy-start.5
  822.8 0.8 copy-start.6
  825.7 431.8 %all-reduce.9.cloned.1.call-start = ((), (), s32[]{:S(2)}) async-start(), calls=%async_computation.3 | async-start | bytes 1048576 | tf_op jit(solution)/shard_map/psum | solution.py:128
  1024.4 2.7 copy-start.1
  1027.1 22.0 %copy-start.12 = (s32[1,8]{1,0:T(1,128)S(1)}, s32[1,8]{1,0:T(1,128)}, u32[]{:S(2)}) copy-start(s32[1,8]{1,0:T(1,128)} %param.32) | copy-start | bytes 100
  1028.4 18.5 %collective-permute-start.6 = (bf16[256,1280]{1,0:T(8,128)(2,1)S(1)}, bf16[256,1280]{1,0:T(8,128)(2,1)S(1)}, u32[]{:S(2)}, u32[]{:S(2)}) collective-permute-start(bf16[256,1280]{1,0:T(8,128)(2,1)S(1)} %get-tuple-element.231), channel_id=1, source_target_pairs={{0,1},{1,2},{2,3},{3,0},{4,5},{5,6},{6,7},{7,4},{8,9},{9,10},{10,1... | collective-permute-start | bytes 1966088 | tf_op jit(solution)/shard_map/ppermute | solution.py:29
  1031.7 18.9 %collective-permute-start.7 = (bf16[256,1280]{1,0:T(8,128)(2,1)S(1)}, bf16[256,1280]{1,0:T(8,128)(2,1)}, u32[]{:S(2)}, u32[]{:S(2)}) collective-permute-start(bf16[256,1280]{1,0:T(8,128)(2,1)S(1)} %get-tuple-element.231), channel_id=1, source_target_pairs={{0,3},{1,0},{2,1},{3,2},{4,7},{5,4},{6,5},{7,6},{8,11},{9,8},{10,9... | collective-permute-start | bytes 1966088 | tf_op jit(solution)/shard_map/ppermute | solution.py:34
  1046.9 17.7 %collective-permute-start.8 = (bf16[256,1280]{1,0:T(8,128)(2,1)S(1)}, bf16[256,1280]{1,0:T(8,128)(2,1)}, u32[]{:S(2)}, u32[]{:S(2)}) collective-permute-start(bf16[256,1280]{1,0:T(8,128)(2,1)S(1)} %collective-permute-done.6), channel_id=1, source_target_pairs={{0,1},{1,2},{2,3},{3,0},{4,5},{5,6},{6,7},{7,4},{8,9},{9,10},{10,1... | collective-permute-start | bytes 1966088 | tf_op jit(solution)/shard_map/ppermute | solution.py:29
  1049.1 17.5 %copy-start.4 = (bf16[40,512]{1,0:T(8,128)(2,1)S(1)}, bf16[40,512]{1,0:T(8,128)(2,1)}, u32[]{:S(2)}) copy-start(bf16[40,512]{1,0:T(8,128)(2,1)} %param.28) | copy-start | bytes 122884
  1050.7 17.9 %copy-start.13 = (s32[8]{0:T(128)S(1)}, s32[8]{0:T(128)}, u32[]{:S(2)}) copy-start(s32[8]{0:T(128)} %select_reduce_fusion) | copy-start | bytes 100
Sparse Core Ops, SparseCore 0:
  616.0 185.5 all-reduce.4
  825.9 198.4 all-reduce.6
  1068.7 188.8 all-reduce.8
